TPU v7x, 32 devices: a whole 2x2x4 slice. The times are simulated.
32 devices in a mesh: tile: 8 (over y, x, core), chan: 4 (over z).
Axes of the slice: x: 2, y: 2, z: 4, core: 2. Of those that a mesh axis runs over, the one named last changes fastest.
Arguments:
- ensemble: bfloat16 [3072, 128, 256], P('tile', 'chan'), may hold values from -6 to 6
- jacobian: bfloat16 [1280, 128, 128], P('tile', 'chan'), may hold values from -1 to 1
- innovation: float32 [1280, 128], P('tile', 'chan'), may hold values from -6 to 6
- error_vectors: float32 [128, 32], replicated, may hold values from -1 to 1, as said below
- error_values: float32 [128], replicated, may hold values from 0.25 to 4
- ensemble_vectors: float32 [256, 256], replicated, may hold values from -1 to 1, as said below
- column_pick: int32 [8, 5, 40], P('tile'), may hold values from 0 to 383
- footprint_slot: int32 [1280], P('tile'), may hold values from 0 to 199, as said below
- footprint_count: int32 [8], P('tile'), may hold values from 20 to 160, as said below
Outputs:
- analysis: bfloat16 [3072, 128, 256], P('tile', 'chan')
Inputs may be any that keep to these rules, and one draw needn't show every extreme that they name: `footprint_slot`: the 160 entries of one pack are distinct; slot o * 40 + j is the j-th column that tile (pack + 2 - o) mod 8 sends to this pack. `footprint_count`: some pack has all 160 footprints live. `error_vectors`: each block of 32 rows is an orthogonal matrix. `ensemble_vectors`: an orthogonal matrix.
All inputs are finite; a program needn't handle non-finite values.
Results may differ from a plain program's by a relative error of at most 0.013.
Values may be sent and summed in bfloat16 or wider, within the bound.
A program may use at most 64 MiB of HBM per device.

v0:
```python
import jax
import jax.numpy as jnp
from jax import lax
from jax.sharding import PartitionSpec as P


def from_behind(value, axis, steps):
    count = lax.axis_size(axis)
    pairs = [(source, (source + steps) % count) for source in range(count)]
    return lax.ppermute(value, axis, pairs)


def turn_blocks(values, vectors):
    row_count, channels, members = values.shape
    group_width = vectors.shape[1]
    grouped = values.reshape(row_count, channels // group_width, group_width, members)
    basis_blocks = vectors.reshape(channels // group_width, group_width, group_width)
    turned = jnp.einsum("gce,fgck->fgek", basis_blocks, grouped, precision=lax.Precision.HIGHEST)
    return turned.reshape(row_count, channels, members)


def turn_rows(values, vectors):
    row_count, channels = values.shape
    group_width = vectors.shape[1]
    grouped = values.reshape(row_count, channels // group_width, group_width)
    basis_blocks = vectors.reshape(channels // group_width, group_width, group_width)
    turned = jnp.einsum("gce,fgc->fge", basis_blocks, grouped, precision=lax.Precision.HIGHEST)
    return turned.reshape(row_count, channels)


def local(
    ensemble,
    jacobian,
    innovation,
    error_vectors,
    error_values,
    ensemble_vectors,
    column_pick,
    footprint_slot,
    footprint_count,
):
    window = column_pick.shape[1]
    capacity = column_pick.shape[2]
    reach_tiles = window // 2
    level_part = ensemble.shape[1]
    members = ensemble.shape[2]
    chosen = jnp.take(ensemble, column_pick[0].reshape(-1), axis=0).reshape(
        window, capacity, level_part, members
    )
    blocks = []
    for slot_index in range(window):
        shift_by = slot_index - reach_tiles
        if shift_by == 0:
            blocks.append(chosen[slot_index])
        else:
            blocks.append(from_behind(chosen[slot_index], "tile", shift_by))
    arrived = jnp.stack(blocks, 0)
    slot_rows = arrived.reshape(window * capacity, level_part, members)
    columns = jnp.take(slot_rows, footprint_slot, axis=0)
    foot_rows = columns.shape[0]
    live_rows = (jnp.arange(foot_rows, dtype=jnp.int32) < footprint_count[0]).astype(jnp.float32)
    share_rows = foot_rows // lax.axis_size("chan")
    columns, sensitivity, misfit_rows = (
        lax.all_to_all(columns, "chan", split_axis=0, concat_axis=1, tiled=True),
        lax.all_to_all(jacobian, "chan", split_axis=0, concat_axis=1, tiled=True),
        lax.all_to_all(
            innovation.astype(jnp.bfloat16), "chan", split_axis=0, concat_axis=1, tiled=True
        ).astype(innovation.dtype),
    )
    response = jnp.einsum("fcl,flk->fck", sensitivity, columns, preferred_element_type=jnp.float32)
    row_weights = lax.dynamic_slice_in_dim(
        live_rows, lax.axis_index("chan") * share_rows, share_rows, 0
    )
    scales = 1.0 / jnp.sqrt(error_values)
    whitened = (
        turn_blocks(response, error_vectors) * scales[None, :, None] * row_weights[:, None, None]
    )
    misfit = turn_rows(misfit_rows, error_vectors) * scales[None, :]
    pull_sum = jnp.einsum("fck,fc->k", whitened, misfit, precision=lax.Precision.HIGHEST)
    rounded = whitened.astype(jnp.bfloat16).reshape(-1, members)
    gram_sum = lax.dot_general(
        rounded, rounded, (((0,), (0,)), ((), ())), preferred_element_type=jnp.float32
    )
    gram_sum, pull_sum = lax.psum((gram_sum, pull_sum), ("tile", "chan"))
    system = gram_sum + (members - 1) * jnp.eye(members, dtype=jnp.float32)
    factor = jnp.linalg.cholesky(system)
    halfway = lax.linalg.triangular_solve(factor, pull_sum[:, None], left_side=True, lower=True)
    mean_weights = lax.linalg.triangular_solve(
        factor, halfway, left_side=True, lower=True, transpose_a=True
    )[:, 0]
    spread = jnp.sqrt(members - 1.0) * lax.linalg.triangular_solve(
        factor, ensemble_vectors, left_side=True, lower=True, transpose_a=True
    )
    transform = (spread + mean_weights[:, None]).astype(jnp.bfloat16)
    flat_rows = ensemble.reshape(-1, members)
    updated = jnp.dot(flat_rows, transform, preferred_element_type=jnp.float32).astype(jnp.bfloat16)
    return updated.reshape(ensemble.shape)


def solution(mesh):
    return jax.shard_map(
        local,
        mesh=mesh,
        in_specs=(
            P("tile", "chan", None),
            P("tile", "chan", None),
            P("tile", "chan"),
            P(),
            P(),
            P(),
            P("tile", None, None),
            P("tile"),
            P("tile"),
        ),
        out_specs=P("tile", "chan", None),
        check_vma=False,
    )
```

profile of v0, /device:TPU:0, one launch (start us, length us, event | category | flops | bytes accessed | tf_op | source)
XLA Modules:
  0.0 357.7 jit_solution(7432755867193582582)
XLA Ops:
  6.5 0.7 reduce.12
  7.4 5.5 %gather_fusion = bf16[200,32,256]{2,1,0:T(8,128)(2,1)} fusion(bf16[384,32,256]{2,1,0:T(8,128)(2,1)} %param.9, s32[1024]{0:T(1024)S(1)} %pad_clamp_fusion.1), kind=kCustom, calls=%fused_computation | custom fusion | bytes 6554400 | tf_op jit(solution)/shard_map/jit(_take)/gather | solution.py:47
  12.9 2.3 broadcast_select_fusion
  15.3 1.5 fusion.43
  16.8 3.9 %collective-permute-start = (bf16[40,32,256]{2,1,0:T(8,128)(2,1)}, bf16[40,32,256]{2,1,0:T(8,128)(2,1)}, u32[]{:S(2)}, u32[]{:S(2)}) collective-permute-start(bf16[40,32,256]{2,1,0:T(8,128)(2,1)} %get-tuple-element.34), channel_id=1, source_target_pairs={{0,24},{4,28},{8,0},{12,4},{16,8},{20,12},{24,16},{28,20},{1,25},{... | collective-permute-start | bytes 1966088 | tf_op jit(solution)/shard_map/ppermute | solution.py:10
  20.7 0.5 collective-permute-start.2
  21.2 0.7 collective-permute-start.3
  22.0 0.7 reshape.193
  22.7 4.9 %all-to-all-start.2 = ((bf16[4,2,640]{2,1,0:T(2,128)(2,1)}), bf16[4,2,640]{2,1,0:T(2,128)(2,1)S(1)}, u32[]{:S(2)}, u32[]{:S(2)}) async-start(bf16[4,2,640]{2,1,0:T(2,128)(2,1)} %reshape.193), calls=%async_computation.2 | async-start | bytes 20480 | tf_op jit(solution)/shard_map/all_to_all | solution.py:66
  27.6 5.6 %all-to-all-done.2 = bf16[4,2,640]{2,1,0:T(2,128)(2,1)S(1)} async-done(((bf16[4,2,640]{2,1,0:T(2,128)(2,1)}), bf16[4,2,640]{2,1,0:T(2,128)(2,1)S(1)}, u32[]{:S(2)}, u32[]{:S(2)}) %all-to-all-start.2) | async-done | bytes 10272 | tf_op jit(solution)/shard_map/all_to_all | solution.py:66
  33.2 4.3 %all-to-all-start.1 = ((bf16[160,32,128]{2,1,0:T(8,128)(2,1)}), bf16[160,32,128]{2,1,0:T(8,128)(2,1)}, u32[]{:S(2)}, u32[]{:S(2)}) async-start(bf16[160,32,128]{2,1,0:T(8,128)(2,1)} %param.10), calls=%async_computation.1 | async-start | bytes 2621440 | tf_op jit(solution)/shard_map/all_to_all | solution.py:65
  37.5 1.1 bitcast_dynamic-update-slice_fusion.4
  38.7 11.5 %collective-permute-done.1 = bf16[40,32,256]{2,1,0:T(8,128)(2,1)} collective-permute-done((bf16[40,32,256]{2,1,0:T(8,128)(2,1)}, bf16[40,32,256]{2,1,0:T(8,128)(2,1)}, u32[]{:S(2)}, u32[]{:S(2)}) %collective-permute-start.1) | collective-permute-done | bytes 655392 | tf_op jit(solution)/shard_map/ppermute | solution.py:10
  50.2 1.1 bitcast_dynamic-update-slice_fusion.3
  51.4 1.1 bitcast_dynamic-update-slice_fusion.2
  52.5 11.6 %collective-permute-done.3 = bf16[40,32,256]{2,1,0:T(8,128)(2,1)} collective-permute-done((bf16[40,32,256]{2,1,0:T(8,128)(2,1)}, bf16[40,32,256]{2,1,0:T(8,128)(2,1)}, u32[]{:S(2)}, u32[]{:S(2)}) %collective-permute-start.3) | collective-permute-done | bytes 655392 | tf_op jit(solution)/shard_map/ppermute | solution.py:10
  64.1 1.1 bitcast_dynamic-update-slice_fusion.1
  65.3 1.7 copy-done.1
  67.0 2.7 gather_fusion.1
  69.7 1.8 broadcast_select_fusion.1
  71.5 5.0 %all-to-all-start = ((bf16[160,32,256]{2,1,0:T(8,128)(2,1)}), bf16[160,32,256]{2,1,0:T(8,128)(2,1)S(1)}, u32[]{:S(2)}, u32[]{:S(2)}) async-start(bf16[160,32,256]{2,1,0:T(8,128)(2,1)} %broadcast_select_fusion.1), calls=%async_computation | async-start | bytes 5242880 | tf_op jit(solution)/shard_map/all_to_all | solution.py:64
  77.9 2.8 copy.24
  80.7 54.4 %all-to-all-done = bf16[160,32,256]{2,1,0:T(8,128)(2,1)S(1)} async-done(((bf16[160,32,256]{2,1,0:T(8,128)(2,1)}), bf16[160,32,256]{2,1,0:T(8,128)(2,1)S(1)}, u32[]{:S(2)}, u32[]{:S(2)}) %all-to-all-start) | async-done | bytes 2621472 | tf_op jit(solution)/shard_map/all_to_all | solution.py:64
  135.1 0.3 copy.23
  135.4 1.0 copy-done
  136.4 0.8 fusion.46
  137.3 6.6 %multiply_convert_fusion = (bf16[40,4,32,256]{3,2,0,1:T(8,128)(2,1)S(1)}, f32[40,4,32,256]{3,2,0,1:T(8,128)}) fusion(f32[40]{0:T(128)S(1)} %dynamic_slice.3, f32[4,32]{1,0:T(4,128)S(1)} %mul.53, f32[4,32,32,1]{1,0,2,3:T(4,128)S(1)} %bitcast.144, f32[40,4,32,256]{3,2,1,0:T(8,128)S(1)} %bitcast.138), kind=kOutput, calls=%fused_computation.10 | convolution fusion | flops 507248640 | bytes 13124256 | tf_op jit(solution)/shard_map/gce,fgck->fgek/dot_general | solution.py:18
  143.9 1.9 fusion.9
  145.8 2.9 copy.35
  148.7 1.1 fusion.1
  149.8 2.7 fusion.45
  152.5 37.0 %psum.15 = f32[256]{0:T(256)S(1)} all-reduce(f32[256]{0:T(256)S(1)} %bitcast.148), channel_id=1, replica_groups=mesh['tile'=8,'chan'=4] {'tile','chan'}, use_global_device_ids=true, to_apply=%region_5.6 | all-reduce | flops 256 | bytes 2048 | tf_op jit(solution)/shard_map/psum | solution.py:84
  189.5 81.2 %all-reduce.3.cloned.1.call-done = f32[256,256]{0,1:T(8,128)} async-done(((f32[256,256]{0,1:T(8,128)}), f32[256,256]{0,1:T(8,128)}) %all-reduce.3.cloned.1.call-update) | async-done | bytes 262160 | tf_op jit(solution)/shard_map/psum | solution.py:84
  270.6 1.0 select_add_fusion
  271.8 1.0 fusion.19
  272.8 11.7 %cholesky.49 = f32[128,128]{1,0:T(8,128)S(1)} custom-call(f32[128,128]{1,0:T(8,128)S(1)} %cholesky.115), custom_call_target="Cholesky" | custom-call | tf_op jit(solution)/shard_map/jit(cholesky)/cholesky | solution.py:86
  284.5 9.8 %custom-call.18 = f32[1,128,128]{1,2,0:T(8,128)S(1)} custom-call(f32[1,128,128]{2,1,0:T(8,128)S(1)} %get-tuple-element.36), custom_call_target="InvertDiagBlocksLowerTriangular" | custom-call | tf_op jit(solution)/shard_map/jit(cholesky)/cholesky | solution.py:86
  294.5 0.3 convolution_subtract_fusion.1
  294.8 11.7 %cholesky.103 = f32[128,128]{1,0:T(8,128)S(1)} custom-call(f32[128,128]{1,0:T(8,128)S(1)} %convolution_subtract_fusion.1), custom_call_target="Cholesky" | custom-call | tf_op jit(solution)/shard_map/jit(cholesky)/cholesky | solution.py:86
  306.9 0.6 compare_reduce_fusion
  308.9 4.0 %while.1 = (s32[]{:T(128)}, f32[256,256]{0,1:T(8,128)S(1)}, s32[2,2]{1,0:T(2,128)S(1)}, f32[2,128,128]{2,1,0:T(8,128)S(1)}, s32[]{:T(128)}) while((s32[]{:T(128)}, f32[256,256]{0,1:T(8,128)S(1)}, s32[2,2]{1,0:T(2,128)S(1)}, f32[2,128,128]{2,1,0:T(8,128)S(1)}, s32[]{:T(128)}) %tuple.27), condition=%wide.while_cond, body=%wide.while_body.sunk | while | flops 2 | bytes 393321 | solution.py:91
  308.9 0.6 fusion.61
  309.5 1.3 dynamic-slice.7
  310.9 0.6 fusion.61
  311.5 1.3 dynamic-slice.7
  312.9 19.9 %custom-call.19 = f32[2,128,128]{1,2,0:T(8,128)S(1)} custom-call(f32[2,128,128]{2,1,0:T(8,128)S(1)} %get-tuple-element.12), custom_call_target="InvertDiagBlocksLowerTriangular" | custom-call | tf_op jit(solution)/shard_map/triangular_solve | solution.py:91
  334.9 7.4 %fusion = bf16[12288,256]{0,1:T(8,128)(2,1)} fusion(bf16[12288,256]{1,0:T(8,128)(2,1)} %bitcast.139, f32[128,256]{1,0:T(8,128)S(1)} %fusion.23, f32[128,256]{1,0:T(8,128)S(1)} %fusion.32, f32[256]{0:T(256)S(1)} %bitcast.147), kind=kOutput, calls=%fused_computation.5 | convolution fusion | flops 1614020608 | bytes 12846080 | tf_op jit(solution)/shard_map/dot_general | solution.py:96
  342.3 8.6 %copy.38 = bf16[12288,256]{1,0:T(8,128)(2,1)} copy(bf16[12288,256]{0,1:T(8,128)(2,1)} %fusion) | data formatting | bytes 12582912 | tf_op jit(solution)/shard_map/convert_element_type | solution.py:96
  (70 shorter events, 4.1 us)
Async XLA Ops:
  15.2 6.7 %copy-start.3 = (f32[160,32]{0,1:T(8,128)S(1)}, f32[160,32]{0,1:T(8,128)}, u32[]{:S(2)}) copy-start(f32[160,32]{0,1:T(8,128)} %param.11) | copy-start | bytes 61444
  15.3 12.4 %copy-start.5 = (s32[160]{0:T(256)S(1)}, s32[160]{0:T(256)}, u32[]{:S(2)}) copy-start(s32[160]{0:T(256)} %param.16) | copy-start | bytes 1924
  16.8 20.7 %collective-permute-start = (bf16[40,32,256]{2,1,0:T(8,128)(2,1)}, bf16[40,32,256]{2,1,0:T(8,128)(2,1)}, u32[]{:S(2)}, u32[]{:S(2)}) collective-permute-start(bf16[40,32,256]{2,1,0:T(8,128)(2,1)} %get-tuple-element.34), channel_id=1, source_target_pairs={{0,24},{4,28},{8,0},{12,4},{16,8},{20,12},{24,16},{28,20},{1,25},{... | collective-permute-start | bytes 1966088 | tf_op jit(solution)/shard_map/ppermute | solution.py:10
  20.7 29.5 %collective-permute-start.1 = (bf16[40,32,256]{2,1,0:T(8,128)(2,1)}, bf16[40,32,256]{2,1,0:T(8,128)(2,1)}, u32[]{:S(2)}, u32[]{:S(2)}) collective-permute-start(bf16[40,32,256]{2,1,0:T(8,128)(2,1)} %get-tuple-element.33), channel_id=1, source_target_pairs={{0,28},{4,0},{8,4},{12,8},{16,12},{20,16},{24,20},{28,24},{1,29},{... | collective-permute-start | bytes 1966088 | tf_op jit(solution)/shard_map/ppermute | solution.py:10
  20.7 30.7 %collective-permute-start.2 = (bf16[40,32,256]{2,1,0:T(8,128)(2,1)}, bf16[40,32,256]{2,1,0:T(8,128)(2,1)}, u32[]{:S(2)}, u32[]{:S(2)}) collective-permute-start(bf16[40,32,256]{2,1,0:T(8,128)(2,1)} %get-tuple-element.32), channel_id=1, source_target_pairs={{0,4},{4,8},{8,12},{12,16},{16,20},{20,24},{24,28},{28,0},{1,5},{5... | collective-permute-start | bytes 1966088 | tf_op jit(solution)/shard_map/ppermute | solution.py:10
  21.2 42.9 %collective-permute-start.3 = (bf16[40,32,256]{2,1,0:T(8,128)(2,1)}, bf16[40,32,256]{2,1,0:T(8,128)(2,1)}, u32[]{:S(2)}, u32[]{:S(2)}) collective-permute-start(bf16[40,32,256]{2,1,0:T(8,128)(2,1)} %get-tuple-element.31), channel_id=1, source_target_pairs={{0,8},{4,12},{8,16},{12,20},{16,24},{20,28},{24,0},{28,4},{1,9},{5... | collective-permute-start | bytes 1966088 | tf_op jit(solution)/shard_map/ppermute | solution.py:10
  22.7 10.5 %all-to-all-start.2 = ((bf16[4,2,640]{2,1,0:T(2,128)(2,1)}), bf16[4,2,640]{2,1,0:T(2,128)(2,1)S(1)}, u32[]{:S(2)}, u32[]{:S(2)}) async-start(bf16[4,2,640]{2,1,0:T(2,128)(2,1)} %reshape.193), calls=%async_computation.2 | async-start | bytes 20480 | tf_op jit(solution)/shard_map/all_to_all | solution.py:66
  33.2 38.3 %all-to-all-start.1 = ((bf16[160,32,128]{2,1,0:T(8,128)(2,1)}), bf16[160,32,128]{2,1,0:T(8,128)(2,1)}, u32[]{:S(2)}, u32[]{:S(2)}) async-start(bf16[160,32,128]{2,1,0:T(8,128)(2,1)} %param.10), calls=%async_computation.1 | async-start | bytes 2621440 | tf_op jit(solution)/shard_map/all_to_all | solution.py:65
  65.2 1.7 copy-start.1
  71.5 5.7 %copy-start.6 = (f32[128]{0:T(128)S(1)}, f32[128]{0:T(128)}, u32[]{:S(2)}) copy-start(f32[128]{0:T(128)} %param.13) | copy-start | bytes 1540
  71.5 5.8 %copy-start.4 = (f32[128,32]{0,1:T(8,128)S(1)}, f32[128,32]{0,1:T(8,128)}, u32[]{:S(2)}) copy-start(f32[128,32]{0,1:T(8,128)} %param.12) | copy-start | bytes 49156
  71.5 63.6 %all-to-all-start = ((bf16[160,32,256]{2,1,0:T(8,128)(2,1)}), bf16[160,32,256]{2,1,0:T(8,128)(2,1)S(1)}, u32[]{:S(2)}, u32[]{:S(2)}) async-start(bf16[160,32,256]{2,1,0:T(8,128)(2,1)} %broadcast_select_fusion.1), calls=%async_computation | async-start | bytes 5242880 | tf_op jit(solution)/shard_map/all_to_all | solution.py:64
  76.5 194.1 %all-reduce.3.cloned.1.call-start = ((), (), s32[]{:S(2)}) async-start(), calls=%async_computation.3 | async-start | bytes 524288 | tf_op jit(solution)/shard_map/psum | solution.py:84
  135.1 1.3 copy-start
  189.5 144.6 %copy-start.2 = (f32[256,256]{1,0:T(8,128)S(1)}, f32[256,256]{1,0:T(8,128)}, u32[]{:S(2)}) copy-start(f32[256,256]{1,0:T(8,128)} %param.14) | copy-start | bytes 786436
Sparse Core Ops, SparseCore 0:
  145.9 124.6 all-reduce.2
where the time goes:
time: 359 us; the launch traced here: 358 us
  waiting for transfers between devices  164 us (46%)
  other arithmetic  61.9 us (17%)
  local copies, waits for them, and re-layouts  37.6 us (10%)
  blocking collectives  37 us (10%)
  matrix products  21.9 us (6%)
  starting transfers between devices  19.3 us (5%)
  between operations  15.6 us (4%)
    psum x1, waiting for transfers between devices, local(): gram_sum, pull_sum = lax.psum((gram_sum, pull_sum), ('tile', 'chan'))  81.2 us
    all_to_all x1, waiting for transfers between devices, local(): lax.all_to_all(columns, 'chan', split_axis=0, concat_axis=1, tiled=True)  54.4 us
    psum x1, blocking collectives, local(): gram_sum, pull_sum = lax.psum((gram_sum, pull_sum), ('tile', 'chan'))  37 us
    another operation x6, other arithmetic, local(): factor = jnp.linalg.cholesky(system)  33.9 us
    ppermute x4, waiting for transfers between devices, from_behind(): return lax.ppermute(value, axis, pairs)  23.1 us
    another operation x3, other arithmetic, local(): lax.linalg.triangular_solve(factor, ensemble_vectors, left_side=True, low...  20 us
    convert_element_type x1, local copies, waits for them, and re-layouts, local(): jnp.dot(flat_rows, transform, preferred_element_type=jnp.float32)  8.6 us
    dot_general x1, matrix products, local(): jnp.dot(flat_rows, transform, preferred_element_type=jnp.float32)  7.38 us
  transfers between devices with their start and end apart: 8, of which 5 were waited for; matrix products, arithmetic and copies ran while one was open for 6% of the time, Pallas kernels for 0%

commit v1 on v0

--- a/solution.py
+++ b/solution.py
@@ -1,7 +1,24 @@
+import functools
 import jax
 import jax.numpy as jnp
 from jax import lax
 from jax.sharding import PartitionSpec as P
+
+
+def fill_the_trees(body, axis_key):
+    o_now = jnp.concatenate(
+        lax.all_to_all(
+            jnp.stack(jnp.split(body, lax.psum(1, axis_name=axis_key), 0)),
+            axis_name=axis_key,
+            split_axis=0,
+            concat_axis=0,
+        ),
+        1,
+    )
+    return o_now
+
+
+form_sources_all_up = functools.partial(fill_the_trees, axis_key="chan")
 
 
 def from_behind(value, axis, steps):
@@ -61,7 +78,7 @@
     live_rows = (jnp.arange(foot_rows, dtype=jnp.int32) < footprint_count[0]).astype(jnp.float32)
     share_rows = foot_rows // lax.axis_size("chan")
     columns, sensitivity, misfit_rows = (
-        lax.all_to_all(columns, "chan", split_axis=0, concat_axis=1, tiled=True),
+        form_sources_all_up(columns),
         lax.all_to_all(jacobian, "chan", split_axis=0, concat_axis=1, tiled=True),
         lax.all_to_all(
             innovation.astype(jnp.bfloat16), "chan", split_axis=0, concat_axis=1, tiled=True

time: 359 us -> 363 us (1.011)
  transfers between devices with their start and end apart: 8 -> 8, of which waited for: 5 -> 5; matrix products, arithmetic and copies ran while one was open for 6% -> 5% of each run, Pallas kernels for 0% -> 0%
where the time goes in v1:
time: 363 us; the launch traced here: 362 us
  waiting for transfers between devices  167 us (46%)
  other arithmetic  65 us (18%)
  blocking collectives  37 us (10%)
  local copies, waits for them, and re-layouts  35.7 us (10%)
  matrix products  22.5 us (6%)
  starting transfers between devices  19.3 us (5%)
  between operations  15.8 us (4%)
    psum x1, waiting for transfers between devices, local(): gram_sum, pull_sum = lax.psum((gram_sum, pull_sum), ('tile', 'chan'))  83.5 us
    all_to_all x1, waiting for transfers between devices, fill_the_trees(): lax.all_to_all(jnp.stack(jnp.split(body, lax.psum(1, axis_name=axis_key),...  54.4 us
    psum x1, blocking collectives, local(): gram_sum, pull_sum = lax.psum((gram_sum, pull_sum), ('tile', 'chan'))  37 us
    another operation x6, other arithmetic, local(): factor = jnp.linalg.cholesky(system)  34 us
    ppermute x4, waiting for transfers between devices, from_behind(): return lax.ppermute(value, axis, pairs)  23.1 us
    another operation x3, other arithmetic, local(): lax.linalg.triangular_solve(factor, ensemble_vectors, left_side=True, low...  20 us
    convert_element_type x1, local copies, waits for them, and re-layouts, local(): jnp.dot(flat_rows, transform, preferred_element_type=jnp.float32)  8.6 us
    dot_general x1, matrix products, local(): jnp.dot(flat_rows, transform, preferred_element_type=jnp.float32)  7.4 us
  transfers between devices with their start and end apart: 8, of which 5 were waited for; matrix products, arithmetic and copies ran while one was open for 5% of the time, Pallas kernels for 0%

profile of v1, /device:TPU:0, one launch (start us, length us, event | category | flops | bytes accessed | tf_op | source)
XLA Modules:
  0.0 361.9 jit_solution(5013113790042947343)
XLA Ops:
  6.5 0.7 reduce.12
  7.4 5.5 %gather_fusion = bf16[200,32,256]{2,1,0:T(8,128)(2,1)} fusion(bf16[384,32,256]{2,1,0:T(8,128)(2,1)} %param.9, s32[1024]{0:T(1024)S(1)} %pad_clamp_fusion.1), kind=kCustom, calls=%fused_computation | custom fusion | bytes 6554400 | tf_op jit(solution)/shard_map/jit(_take)/gather | solution.py:64
  12.9 2.3 broadcast_select_fusion
  15.3 1.5 fusion.43
  16.8 3.9 %collective-permute-start = (bf16[40,32,256]{2,1,0:T(8,128)(2,1)}, bf16[40,32,256]{2,1,0:T(8,128)(2,1)}, u32[]{:S(2)}, u32[]{:S(2)}) collective-permute-start(bf16[40,32,256]{2,1,0:T(8,128)(2,1)} %get-tuple-element.38), channel_id=1, source_target_pairs={{0,24},{4,28},{8,0},{12,4},{16,8},{20,12},{24,16},{28,20},{1,25},{... | collective-permute-start | bytes 1966088 | tf_op jit(solution)/shard_map/ppermute | solution.py:27
  20.7 0.5 collective-permute-start.2
  21.2 0.7 collective-permute-start.3
  22.0 0.7 reshape.201
  22.7 4.9 %all-to-all-start.2 = ((bf16[4,2,640]{2,1,0:T(2,128)(2,1)}), bf16[4,2,640]{2,1,0:T(2,128)(2,1)S(1)}, u32[]{:S(2)}, u32[]{:S(2)}) async-start(bf16[4,2,640]{2,1,0:T(2,128)(2,1)} %reshape.201), calls=%async_computation.2 | async-start | bytes 20480 | tf_op jit(solution)/shard_map/all_to_all | solution.py:83
  27.6 5.6 %all-to-all-done.2 = bf16[4,2,640]{2,1,0:T(2,128)(2,1)S(1)} async-done(((bf16[4,2,640]{2,1,0:T(2,128)(2,1)}), bf16[4,2,640]{2,1,0:T(2,128)(2,1)S(1)}, u32[]{:S(2)}, u32[]{:S(2)}) %all-to-all-start.2) | async-done | bytes 10272 | tf_op jit(solution)/shard_map/all_to_all | solution.py:83
  33.2 4.3 %all-to-all-start.1 = ((bf16[160,32,128]{2,1,0:T(8,128)(2,1)}), bf16[160,32,128]{2,1,0:T(8,128)(2,1)}, u32[]{:S(2)}, u32[]{:S(2)}) async-start(bf16[160,32,128]{2,1,0:T(8,128)(2,1)} %param.10), calls=%async_computation.1 | async-start | bytes 2621440 | tf_op jit(solution)/shard_map/all_to_all | solution.py:82
  37.5 1.1 bitcast_dynamic-update-slice_fusion.4
  38.7 11.5 %collective-permute-done.1 = bf16[40,32,256]{2,1,0:T(8,128)(2,1)} collective-permute-done((bf16[40,32,256]{2,1,0:T(8,128)(2,1)}, bf16[40,32,256]{2,1,0:T(8,128)(2,1)}, u32[]{:S(2)}, u32[]{:S(2)}) %collective-permute-start.1) | collective-permute-done | bytes 655392 | tf_op jit(solution)/shard_map/ppermute | solution.py:27
  50.2 1.1 bitcast_dynamic-update-slice_fusion.3
  51.4 1.1 bitcast_dynamic-update-slice_fusion.2
  52.5 11.6 %collective-permute-done.3 = bf16[40,32,256]{2,1,0:T(8,128)(2,1)} collective-permute-done((bf16[40,32,256]{2,1,0:T(8,128)(2,1)}, bf16[40,32,256]{2,1,0:T(8,128)(2,1)}, u32[]{:S(2)}, u32[]{:S(2)}) %collective-permute-start.3) | collective-permute-done | bytes 655392 | tf_op jit(solution)/shard_map/ppermute | solution.py:27
  64.1 1.1 bitcast_dynamic-update-slice_fusion.1
  65.3 1.7 copy-done.1
  67.0 2.7 gather_fusion.1
  69.7 0.3 broadcast_select_fusion.1
  70.0 0.3 slice_bitcast_fusion.3
  70.3 1.8 pad_maximum_fusion
  72.1 5.0 %all-to-all-start = ((bf16[4,40,32,256]{3,2,1,0:T(8,128)(2,1)}), bf16[4,40,32,256]{3,2,1,0:T(8,128)(2,1)S(1)}, u32[]{:S(2)}, u32[]{:S(2)}) async-start(bf16[4,40,32,256]{3,2,1,0:T(8,128)(2,1)} %pad_maximum_fusion), calls=%async_computation | async-start | bytes 5242880 | tf_op jit(solution)/shard_map/all_to_all | solution.py:10
  78.5 2.8 copy.45
  81.3 54.4 %all-to-all-done = bf16[4,40,32,256]{3,2,1,0:T(8,128)(2,1)S(1)} async-done(((bf16[4,40,32,256]{3,2,1,0:T(8,128)(2,1)}), bf16[4,40,32,256]{3,2,1,0:T(8,128)(2,1)S(1)}, u32[]{:S(2)}, u32[]{:S(2)}) %all-to-all-start) | async-done | bytes 2621472 | tf_op jit(solution)/shard_map/all_to_all | solution.py:10
  136.0 1.0 copy-done
  137.0 0.8 fusion.46
  137.9 5.5 %multiply_convert_fusion = (bf16[40,4,32,256]{3,2,0,1:T(8,128)(2,1)S(1)}, f32[40,4,32,256]{3,2,0,1:T(8,128)S(1)}) fusion(f32[40]{0:T(128)S(1)} %dynamic_slice.3, f32[4,32]{1,0:T(4,128)S(1)} %mul.53, f32[4,32,32,1]{1,0,2,3:T(4,128)S(1)} %bitcast.150, f32[40,4,32,256]{3,2,1,0:T(8,128)S(1)} %bitcast.144), kind=kOutput, calls=%fused_computation.10 | convolution fusion | flops 507248640 | bytes 13124256 | tf_op jit(solution)/shard_map/gce,fgck->fgek/dot_general | solution.py:35
  143.4 0.4 copy.56
  143.8 3.7 %fusion.1 = f32[40,128,256]{2,1,0:T(8,128)} fusion(f32[40,4,32,256]{3,2,1,0:T(8,128)S(1)} %copy.56, f32[40]{0:T(128)S(1)} %dynamic_slice.3, f32[128]{0:T(128)S(1)} %sqrt.3), kind=kLoop, calls=%fused_computation.7 | loop fusion | flops 2621440 | bytes 10486432 | tf_op jit(solution)/shard_map/mul | solution.py:93
  147.5 1.9 fusion.9
  149.5 4.4 %fusion.45 = f32[1,256,1]{1,0,2:T(1,128)S(1)} fusion(f32[40,128,256]{2,1,0:T(8,128)} %fusion.1, f32[40,128,1]{1,2,0:T(1,128)S(1)} %copy.62), kind=kOutput, calls=%fused_computation.95 | convolution fusion | flops 15728640 | bytes 5264384 | tf_op jit(solution)/shard_map/fck,fc->k/dot_general | solution.py:96
  153.8 37.0 %psum.15 = f32[256]{0:T(256)S(1)} all-reduce(f32[256]{0:T(256)S(1)} %bitcast.154), channel_id=1, replica_groups=mesh['tile'=8,'chan'=4] {'tile','chan'}, use_global_device_ids=true, to_apply=%region_5.6 | all-reduce | flops 256 | bytes 2048 | tf_op jit(solution)/shard_map/psum | solution.py:101
  190.9 83.5 %all-reduce.3.cloned.1.call-done = f32[256,256]{0,1:T(8,128)} async-done(((f32[256,256]{0,1:T(8,128)}), f32[256,256]{0,1:T(8,128)}) %all-reduce.3.cloned.1.call-update) | async-done | bytes 262160 | tf_op jit(solution)/shard_map/psum | solution.py:101
  274.4 1.0 select_add_fusion
  275.5 1.0 fusion.19
  276.5 11.7 %cholesky.49 = f32[128,128]{1,0:T(8,128)S(1)} custom-call(f32[128,128]{1,0:T(8,128)S(1)} %cholesky.115), custom_call_target="Cholesky" | custom-call | tf_op jit(solution)/shard_map/jit(cholesky)/cholesky | solution.py:103
  288.2 9.8 %custom-call.18 = f32[1,128,128]{1,2,0:T(8,128)S(1)} custom-call(f32[1,128,128]{2,1,0:T(8,128)S(1)} %get-tuple-element.44), custom_call_target="InvertDiagBlocksLowerTriangular" | custom-call | tf_op jit(solution)/shard_map/jit(cholesky)/cholesky | solution.py:103
  298.5 11.7 %cholesky.103 = f32[128,128]{1,0:T(8,128)S(1)} custom-call(f32[128,128]{1,0:T(8,128)S(1)} %convolution_subtract_fusion.1), custom_call_target="Cholesky" | custom-call | tf_op jit(solution)/shard_map/jit(cholesky)/cholesky | solution.py:103
  310.6 0.7 compare_reduce_fusion
  312.8 4.3 %while.1 = (s32[]{:T(128)}, f32[256,256]{0,1:T(8,128)S(1)}, s32[2,2]{1,0:T(2,128)S(1)}, f32[2,128,128]{2,1,0:T(8,128)S(1)}, s32[]{:T(128)}) while((s32[]{:T(128)}, f32[256,256]{0,1:T(8,128)S(1)}, s32[2,2]{1,0:T(2,128)S(1)}, f32[2,128,128]{2,1,0:T(8,128)S(1)}, s32[]{:T(128)}) %tuple.31), condition=%wide.while_cond, body=%wide.while_body.sunk | while | flops 2 | bytes 393321 | solution.py:108
  312.8 0.6 fusion.61
  313.4 1.4 dynamic-slice.7
  315.0 0.6 fusion.61
  315.6 1.4 dynamic-slice.7
  317.2 19.9 %custom-call.19 = f32[2,128,128]{1,2,0:T(8,128)S(1)} custom-call(f32[2,128,128]{2,1,0:T(8,128)S(1)} %get-tuple-element.12), custom_call_target="InvertDiagBlocksLowerTriangular" | custom-call | tf_op jit(solution)/shard_map/triangular_solve | solution.py:108
  339.1 7.4 %fusion = bf16[12288,256]{0,1:T(8,128)(2,1)} fusion(bf16[12288,256]{1,0:T(8,128)(2,1)} %bitcast.145, f32[128,256]{1,0:T(8,128)S(1)} %fusion.23, f32[128,256]{1,0:T(8,128)S(1)} %fusion.32, f32[256]{0:T(256)S(1)} %bitcast.153), kind=kOutput, calls=%fused_computation.5 | convolution fusion | flops 1614020608 | bytes 12846080 | tf_op jit(solution)/shard_map/dot_general | solution.py:113
  346.5 8.6 %copy.59 = bf16[12288,256]{1,0:T(8,128)(2,1)} copy(bf16[12288,256]{0,1:T(8,128)(2,1)} %fusion) | data formatting | bytes 12582912 | tf_op jit(solution)/shard_map/convert_element_type | solution.py:113
  (72 shorter events, 4.6 us)
Async XLA Ops:
  15.2 6.7 %copy-start.3 = (f32[160,32]{0,1:T(8,128)S(1)}, f32[160,32]{0,1:T(8,128)}, u32[]{:S(2)}) copy-start(f32[160,32]{0,1:T(8,128)} %param.11) | copy-start | bytes 61444
  15.3 12.4 %copy-start.5 = (s32[160]{0:T(256)S(1)}, s32[160]{0:T(256)}, u32[]{:S(2)}) copy-start(s32[160]{0:T(256)} %param.16) | copy-start | bytes 1924
  16.8 20.7 %collective-permute-start = (bf16[40,32,256]{2,1,0:T(8,128)(2,1)}, bf16[40,32,256]{2,1,0:T(8,128)(2,1)}, u32[]{:S(2)}, u32[]{:S(2)}) collective-permute-start(bf16[40,32,256]{2,1,0:T(8,128)(2,1)} %get-tuple-element.38), channel_id=1, source_target_pairs={{0,24},{4,28},{8,0},{12,4},{16,8},{20,12},{24,16},{28,20},{1,25},{... | collective-permute-start | bytes 1966088 | tf_op jit(solution)/shard_map/ppermute | solution.py:27
  20.7 29.5 %collective-permute-start.1 = (bf16[40,32,256]{2,1,0:T(8,128)(2,1)}, bf16[40,32,256]{2,1,0:T(8,128)(2,1)}, u32[]{:S(2)}, u32[]{:S(2)}) collective-permute-start(bf16[40,32,256]{2,1,0:T(8,128)(2,1)} %get-tuple-element.37), channel_id=1, source_target_pairs={{0,28},{4,0},{8,4},{12,8},{16,12},{20,16},{24,20},{28,24},{1,29},{... | collective-permute-start | bytes 1966088 | tf_op jit(solution)/shard_map/ppermute | solution.py:27
  20.7 30.7 %collective-permute-start.2 = (bf16[40,32,256]{2,1,0:T(8,128)(2,1)}, bf16[40,32,256]{2,1,0:T(8,128)(2,1)}, u32[]{:S(2)}, u32[]{:S(2)}) collective-permute-start(bf16[40,32,256]{2,1,0:T(8,128)(2,1)} %get-tuple-element.36), channel_id=1, source_target_pairs={{0,4},{4,8},{8,12},{12,16},{16,20},{20,24},{24,28},{28,0},{1,5},{5... | collective-permute-start | bytes 1966088 | tf_op jit(solution)/shard_map/ppermute | solution.py:27
  21.2 42.9 %collective-permute-start.3 = (bf16[40,32,256]{2,1,0:T(8,128)(2,1)}, bf16[40,32,256]{2,1,0:T(8,128)(2,1)}, u32[]{:S(2)}, u32[]{:S(2)}) collective-permute-start(bf16[40,32,256]{2,1,0:T(8,128)(2,1)} %get-tuple-element.35), channel_id=1, source_target_pairs={{0,8},{4,12},{8,16},{12,20},{16,24},{20,28},{24,0},{28,4},{1,9},{5... | collective-permute-start | bytes 1966088 | tf_op jit(solution)/shard_map/ppermute | solution.py:27
  22.7 10.5 %all-to-all-start.2 = ((bf16[4,2,640]{2,1,0:T(2,128)(2,1)}), bf16[4,2,640]{2,1,0:T(2,128)(2,1)S(1)}, u32[]{:S(2)}, u32[]{:S(2)}) async-start(bf16[4,2,640]{2,1,0:T(2,128)(2,1)} %reshape.201), calls=%async_computation.2 | async-start | bytes 20480 | tf_op jit(solution)/shard_map/all_to_all | solution.py:83
  33.2 38.9 %all-to-all-start.1 = ((bf16[160,32,128]{2,1,0:T(8,128)(2,1)}), bf16[160,32,128]{2,1,0:T(8,128)(2,1)}, u32[]{:S(2)}, u32[]{:S(2)}) async-start(bf16[160,32,128]{2,1,0:T(8,128)(2,1)} %param.10), calls=%async_computation.1 | async-start | bytes 2621440 | tf_op jit(solution)/shard_map/all_to_all | solution.py:82
  65.2 1.7 copy-start.1
  72.1 5.7 %copy-start.6 = (f32[128]{0:T(128)S(1)}, f32[128]{0:T(128)}, u32[]{:S(2)}) copy-start(f32[128]{0:T(128)} %param.13) | copy-start | bytes 1540
  72.1 5.8 %copy-start.4 = (f32[128,32]{0,1:T(8,128)S(1)}, f32[128,32]{0,1:T(8,128)}, u32[]{:S(2)}) copy-start(f32[128,32]{0,1:T(8,128)} %param.12) | copy-start | bytes 49156
  72.1 63.6 %all-to-all-start = ((bf16[4,40,32,256]{3,2,1,0:T(8,128)(2,1)}), bf16[4,40,32,256]{3,2,1,0:T(8,128)(2,1)S(1)}, u32[]{:S(2)}, u32[]{:S(2)}) async-start(bf16[4,40,32,256]{3,2,1,0:T(8,128)(2,1)} %pad_maximum_fusion), calls=%async_computation | async-start | bytes 5242880 | tf_op jit(solution)/shard_map/all_to_all | solution.py:10
  77.2 197.2 %all-reduce.3.cloned.1.call-start = ((), (), s32[]{:S(2)}) async-start(), calls=%async_computation.3 | async-start | bytes 524288 | tf_op jit(solution)/shard_map/psum | solution.py:101
  135.7 1.3 copy-start
  190.9 147.4 %copy-start.2 = (f32[256,256]{1,0:T(8,128)S(1)}, f32[256,256]{1,0:T(8,128)}, u32[]{:S(2)}) copy-start(f32[256,256]{1,0:T(8,128)} %param.14) | copy-start | bytes 786436
Sparse Core Ops, SparseCore 0:
  149.6 124.7 all-reduce.2
